TPU v7x, 32 devices: a whole 2x2x4 slice. The times are simulated.
32 devices in a mesh: grp: 4 (over x, core), tp: 8 (over z, y).
Axes of the slice: x: 2, y: 2, z: 4, core: 2. Of those that a mesh axis runs over, the one named last changes fastest.
Arguments:
- tokens: bfloat16 [3072, 8192], P(('grp', 'tp')), may hold values from -6 to 6
- holder: int32 [3072, 1], P(('grp', 'tp')), may hold values from 0 to 31; in each aligned block of 96 rows (0 to 95, 96 to 191, ...) at most 6 rows name the same one
- adapter_choice_index: int32 [3072, 1], P(('grp', 'tp')), may hold values from 0 to 1
- query_base_output: bfloat16 [8192, 8192], P(None, 'tp'), may hold values from -0.0625 to 0.0625
- value_base_output: bfloat16 [8192, 1024], P(None, 'tp'), may hold values from -0.0625 to 0.0625
- adapter_down_weight: bfloat16 [64, 8192, 128], P(('grp', 'tp')), may hold values from -0.0625 to 0.0625
- adapter_query_up: bfloat16 [64, 64, 8192], P(('grp', 'tp')), may hold values from -0.75 to 0.75
- adapter_value_up: bfloat16 [64, 64, 1024], P(('grp', 'tp')), may hold values from -0.75 to 0.75
Outputs:
- queries: bfloat16 [3072, 8192], P(('grp', 'tp'))
- values: bfloat16 [3072, 1024], P(('grp', 'tp'))
Inputs may be any that keep to these rules, and one draw needn't show every extreme that they name: Among the 96 requests of one device no holder appears more than 6 times, and some holder appears exactly 6 times.
All inputs are finite; a program needn't handle non-finite values.
Results may differ from a plain program's by a relative error of at most 0.0057.
Values may be sent and summed in bfloat16 or wider, within the bound.
A program may use at most 128 MiB of HBM per device.

v0:
```python
import jax
import jax.numpy as jnp
from jax import lax
from jax.sharding import PartitionSpec as P

adapter_scale = 2.0


def apply_lowrank_adapters(
    flattened_rows, flattened_metadata, adapter_down_weight, adapter_query_up, adapter_value_up
):
    adapter_weights = adapter_down_weight.shape[0]
    rank_size = adapter_query_up.shape[1]
    slot_count = flattened_rows.shape[0]
    reduced_state = jnp.einsum(
        "ct,ztw->czw", flattened_rows, adapter_down_weight, preferred_element_type=jnp.float32
    )
    keep_mask = (
        flattened_metadata.astype(jnp.float32)[:, None]
        == jnp.arange(adapter_weights, dtype=jnp.float32)[None, :]
    )
    reduced_state = jnp.where(keep_mask[:, :, None], reduced_state, 0.0).astype(jnp.bfloat16)
    query_reduced = reduced_state[:, :, :rank_size].reshape(slot_count, adapter_weights * rank_size)
    value_reduced = reduced_state[:, :, rank_size:].reshape(slot_count, adapter_weights * rank_size)
    flattened_query_up = adapter_query_up.reshape(
        adapter_weights * rank_size, adapter_query_up.shape[2]
    )
    flattened_value_up = adapter_value_up.reshape(
        adapter_weights * rank_size, adapter_value_up.shape[2]
    )
    query_correction = (
        adapter_scale
        * jnp.dot(query_reduced, flattened_query_up, preferred_element_type=jnp.float32)
    ).astype(jnp.bfloat16)
    value_correction = (
        adapter_scale
        * jnp.dot(value_reduced, flattened_value_up, preferred_element_type=jnp.float32)
    ).astype(jnp.bfloat16)
    return (query_correction, value_correction)


def on_device(
    tokens,
    holder,
    adapter_choice_index,
    query_base_output,
    value_base_output,
    adapter_down_weight,
    adapter_query_up,
    adapter_value_up,
):
    row_count, width = tokens.shape
    query_cols = query_base_output.shape[1]
    piece = lax.all_gather(tokens, "tp", axis=0, tiled=True)
    part_query = jnp.dot(piece, query_base_output, preferred_element_type=jnp.float32).astype(
        jnp.bfloat16
    )
    part_value = jnp.dot(piece, value_base_output, preferred_element_type=jnp.float32).astype(
        jnp.bfloat16
    )
    projected = jnp.concatenate([part_query, part_value], axis=1)
    plain_query, plain_value = (
        lax.all_to_all(projected[:, :query_cols], "tp", split_axis=0, concat_axis=1, tiled=True),
        lax.all_to_all(projected[:, query_cols:], "tp", split_axis=0, concat_axis=1, tiled=True),
    )
    groups = lax.axis_size("grp")
    members = lax.axis_size("tp")
    devices = groups * members
    capacity = max(2, 2 * row_count // devices)
    slot_total = devices * capacity
    holder_id = holder[:, 0]
    same_holder = holder_id[:, None] == holder_id[None, :]
    earlier = (
        jnp.arange(row_count, dtype=jnp.int32)[:, None]
        > jnp.arange(row_count, dtype=jnp.int32)[None, :]
    )
    position = jnp.sum((same_holder & earlier).astype(jnp.int32), axis=1)
    slot_index = holder_id * capacity + position
    pick_table = (jnp.arange(slot_total, dtype=jnp.int32)[:, None] == slot_index[None, :]).astype(
        jnp.bfloat16
    )
    send_rows = jnp.dot(pick_table, tokens, preferred_element_type=jnp.float32).astype(jnp.bfloat16)
    send_meta = jnp.dot(
        pick_table, adapter_choice_index.astype(jnp.bfloat16), preferred_element_type=jnp.float32
    )
    send_meta = send_meta[:, 0].astype(jnp.bfloat16)
    got_rows = lax.all_to_all(
        send_rows.reshape(devices, capacity, width),
        ("grp", "tp"),
        split_axis=0,
        concat_axis=0,
        tiled=True,
    )
    got_meta = lax.all_to_all(
        send_meta.reshape(devices, capacity), ("grp", "tp"), split_axis=0, concat_axis=0, tiled=True
    )
    lead, items = got_meta.shape
    query_correction, value_correction = apply_lowrank_adapters(
        got_rows.reshape(lead * items, width),
        got_meta.reshape(lead * items),
        adapter_down_weight,
        adapter_query_up,
        adapter_value_up,
    )
    back_query = lax.all_to_all(
        query_correction.reshape(lead, items, query_correction.shape[1]),
        ("grp", "tp"),
        split_axis=0,
        concat_axis=0,
        tiled=True,
    )
    back_value = lax.all_to_all(
        value_correction.reshape(lead, items, value_correction.shape[1]),
        ("grp", "tp"),
        split_axis=0,
        concat_axis=0,
        tiled=True,
    )
    flat_query = back_query.reshape(slot_total, back_query.shape[-1])
    flat_value = back_value.reshape(slot_total, back_value.shape[-1])
    row_query = jnp.take(flat_query, slot_index, axis=0)
    row_value = jnp.take(flat_value, slot_index, axis=0)
    queries = (plain_query.astype(jnp.float32) + row_query.astype(jnp.float32)).astype(jnp.bfloat16)
    values = (plain_value.astype(jnp.float32) + row_value.astype(jnp.float32)).astype(jnp.bfloat16)
    return (queries, values)


def solution(mesh):
    return jax.shard_map(
        on_device,
        mesh=mesh,
        in_specs=(
            P(("grp", "tp"), None),
            P(("grp", "tp"), None),
            P(("grp", "tp"), None),
            P(None, "tp"),
            P(None, "tp"),
            P(("grp", "tp"), None, None),
            P(("grp", "tp"), None, None),
            P(("grp", "tp"), None, None),
        ),
        out_specs=(P(("grp", "tp"), None), P(("grp", "tp"), None)),
        check_vma=False,
    )
```

profile of v0, /device:TPU:13, one launch (start us, length us, event | category | flops | bytes accessed | tf_op | source)
XLA Modules:
  0.0 444.6 jit_solution(4456755326801839803)
XLA Ops:
  7.2 0.0 copy-start
  7.2 0.0 all-gather.2.cloned.1.call-start
  7.2 0.7 all-gather.2.cloned.1.call-update
  7.9 0.9 convert_reduce_fusion
  8.8 0.7 multiply_add_fusion.1
  9.5 0.1 broadcast_compare_fusion
  9.6 0.8 fusion.8
  10.4 0.1 copy.33
  10.5 0.7 copy.28
  11.3 6.3 %all-to-all-start.1 = ((bf16[32,1,6]{2,1,0:T(2,128)(2,1)}), bf16[32,1,6]{2,1,0:T(2,128)(2,1)S(1)}, u32[]{:S(2)}, u32[]{:S(2)}) async-start(bf16[32,1,6]{2,1,0:T(2,128)(2,1)} %copy.28), calls=%async_computation.1 | async-start | bytes 32768 | tf_op jit(solution)/shard_map/all_to_all | solution.py:94
  17.5 4.0 convolution_convert_fusion
  21.6 4.9 %reshape.110 = bf16[32,6,8192]{2,1,0:T(8,128)(2,1)} reshape(bf16[192,8192]{1,0:T(8,128)(2,1)} %convolution_convert_fusion) | data formatting | bytes 6291456 | tf_op jit(solution)/shard_map/reshape | solution.py:88
  26.5 0.0 all-to-all-done.1
  26.5 5.9 %all-to-all-start.2 = ((bf16[32,6,8192]{2,1,0:T(8,128)(2,1)}), bf16[32,6,8192]{2,1,0:T(8,128)(2,1)}, u32[]{:S(2)}, u32[]{:S(2)}) async-start(bf16[32,6,8192]{2,1,0:T(8,128)(2,1)} %reshape.110), calls=%async_computation.2 | async-start | bytes 8388608 | tf_op jit(solution)/shard_map/all_to_all | solution.py:87
  32.5 0.1 convert_reduce_fusion.1
  32.5 0.1 reshape.117
  32.6 185.1 %all-to-all-done.2 = bf16[32,6,8192]{2,1,0:T(8,128)(2,1)} async-done(((bf16[32,6,8192]{2,1,0:T(8,128)(2,1)}), bf16[32,6,8192]{2,1,0:T(8,128)(2,1)}, u32[]{:S(2)}, u32[]{:S(2)}) %all-to-all-start.2) | async-done | bytes 3145760 | tf_op jit(solution)/shard_map/all_to_all | solution.py:87
  217.7 5.0 %reshape.137 = bf16[192,8192,1]{1,0,2:T(8,128)(2,1)} reshape(bf16[32,6,8192]{2,1,0:T(8,128)(2,1)} %all-to-all-done.2) | data formatting | bytes 6291456 | tf_op jit(solution)/shard_map/reshape | solution.py:99
  222.7 0.0 copy-start.3
  222.7 4.2 fusion.4
  226.9 0.0 copy-done.3
  226.9 0.4 fusion.3
  227.3 0.9 reshape.114
  228.3 6.7 %all-to-all-start.5 = ((bf16[32,6,1024]{2,1,0:T(8,128)(2,1)}), bf16[32,6,1024]{2,1,0:T(8,128)(2,1)S(1)}, u32[]{:S(2)}, u32[]{:S(2)}) async-start(bf16[32,6,1024]{2,1,0:T(8,128)(2,1)} %reshape.114), calls=%async_computation.5 | async-start | bytes 1048576 | tf_op jit(solution)/shard_map/all_to_all | solution.py:112
  235.0 0.0 copy-done
  235.0 2.7 fusion.1
  237.6 4.9 %reshape.112 = bf16[32,6,8192]{2,1,0:T(8,128)(2,1)} reshape(bf16[192,8192]{1,0:T(8,128)(2,1)} %fusion.1) | data formatting | bytes 6291456 | tf_op jit(solution)/shard_map/reshape | solution.py:106
  242.5 0.0 copy-start.5
  242.5 18.3 %all-to-all-done.5 = bf16[32,6,1024]{2,1,0:T(8,128)(2,1)S(1)} async-done(((bf16[32,6,1024]{2,1,0:T(8,128)(2,1)}), bf16[32,6,1024]{2,1,0:T(8,128)(2,1)S(1)}, u32[]{:S(2)}, u32[]{:S(2)}) %all-to-all-start.5) | async-done | bytes 393248 | tf_op jit(solution)/shard_map/all_to_all | solution.py:112
  260.9 8.4 %all-to-all-start.3 = ((bf16[32,6,8192]{2,1,0:T(8,128)(2,1)}), bf16[32,6,8192]{2,1,0:T(8,128)(2,1)}, u32[]{:S(2)}, u32[]{:S(2)}) async-start(bf16[32,6,8192]{2,1,0:T(8,128)(2,1)} %reshape.112), calls=%async_computation.3 | async-start | bytes 8388608 | tf_op jit(solution)/shard_map/all_to_all | solution.py:105
  269.3 40.0 %all-gather.2.cloned.1.call-done = bf16[768,8192]{1,0:T(8,128)(2,1)} async-done(((bf16[96,8192]{1,0:T(8,128)(2,1)}), bf16[768,8192]{1,0:T(8,128)(2,1)}) %all-gather.2.cloned.1.call-update) | async-done | bytes 12582928 | tf_op jit(solution)/shard_map/all_gather | solution.py:54
  309.3 0.0 copy-done.5
  309.3 7.1 %convolution_convert_fusion.2 = bf16[768,128]{1,0:T(8,128)(2,1)} fusion(bf16[768,8192]{1,0:T(8,128)(2,1)} %all-gather.2.cloned.1.call-done, bf16[8192,128]{1,0:T(8,128)(2,1)S(1)} %copy-done.5), kind=kOutput, calls=%fused_computation.12 | convolution fusion | flops 1610711040 | bytes 14876672 | tf_op jit(solution)/shard_map/dot_general | solution.py:58
  316.4 49.6 %all-to-all-done.3 = bf16[32,6,8192]{2,1,0:T(8,128)(2,1)} async-done(((bf16[32,6,8192]{2,1,0:T(8,128)(2,1)}), bf16[32,6,8192]{2,1,0:T(8,128)(2,1)}, u32[]{:S(2)}, u32[]{:S(2)}) %all-to-all-start.3) | async-done | bytes 3145760 | tf_op jit(solution)/shard_map/all_to_all | solution.py:105
  366.0 7.0 %all-to-all-start.4 = ((bf16[8,96,128]{2,1,0:T(8,128)(2,1)}), bf16[8,96,128]{2,1,0:T(8,128)(2,1)S(1)}, u32[]{:S(2)}, u32[]{:S(2)}) async-start(bf16[8,96,128]{2,1,0:T(8,128)(2,1)} %bitcast.11), calls=%async_computation.4 | async-start | bytes 393216 | tf_op jit(solution)/shard_map/all_to_all | solution.py:64
  373.0 19.9 %convolution_convert_fusion.1 = bf16[768,1024]{1,0:T(8,128)(2,1)} fusion(bf16[768,8192]{1,0:T(8,128)(2,1)} %all-gather.2.cloned.1.call-done, bf16[8192,1024]{1,0:T(8,128)(2,1)} %param.11), kind=kOutput, calls=%fused_computation.8 | convolution fusion | flops 12885688320 | bytes 30932992 | tf_op jit(solution)/shard_map/dot_general | solution.py:55
  392.9 0.0 copy-start.4
  392.9 0.0 all-to-all-done.4
  392.9 5.6 %all-to-all-start = ((bf16[8,96,1024]{2,1,0:T(8,128)(2,1)}), bf16[8,96,1024]{2,1,0:T(8,128)(2,1)}, u32[]{:S(2)}, u32[]{:S(2)}) async-start(bf16[8,96,1024]{2,1,0:T(8,128)(2,1)} %bitcast), calls=%async_computation | async-start | bytes 3145728 | tf_op jit(solution)/shard_map/all_to_all | solution.py:63
  398.5 0.0 copy-done.4
  398.5 0.1 reshape.115
  398.7 0.8 gather_fusion.1
  399.4 3.4 reshape.113
  402.9 2.7 gather_fusion
  405.6 0.8 fusion.5
  406.4 26.5 %all-to-all-done = bf16[8,96,1024]{2,1,0:T(8,128)(2,1)} async-done(((bf16[8,96,1024]{2,1,0:T(8,128)(2,1)}), bf16[8,96,1024]{2,1,0:T(8,128)(2,1)}, u32[]{:S(2)}, u32[]{:S(2)}) %all-to-all-start) | async-done | bytes 1572896 | tf_op jit(solution)/shard_map/all_to_all | solution.py:63
  432.9 1.8 convert_bitcast_fusion
  434.7 0.0 copy-start.2
  434.7 0.4 copy.36
  435.1 0.0 copy-start.1
  435.1 1.0 copy-done.2
  436.1 1.6 add_convert_fusion
  437.7 0.0 copy-done.1
  (5 shorter events, 0.0 us)
Async XLA Ops:
  7.2 227.8 %copy-start = (bf16[2,64,8192]{2,1,0:T(8,128)(2,1)S(1)}, bf16[2,64,8192]{2,1,0:T(8,128)(2,1)}, u32[]{:S(2)}) copy-start(bf16[2,64,8192]{2,1,0:T(8,128)(2,1)} %param.14) | copy-start | bytes 6291460
  7.2 302.1 %all-gather.2.cloned.1.call-start = ((), (), s32[]{:S(2)}) async-start(), calls=%async_computation.6 | async-start | bytes 14155776 | tf_op jit(solution)/shard_map/all_gather | solution.py:54
  11.3 15.2 %all-to-all-start.1 = ((bf16[32,1,6]{2,1,0:T(2,128)(2,1)}), bf16[32,1,6]{2,1,0:T(2,128)(2,1)S(1)}, u32[]{:S(2)}, u32[]{:S(2)}) async-start(bf16[32,1,6]{2,1,0:T(2,128)(2,1)} %copy.28), calls=%async_computation.1 | async-start | bytes 32768 | tf_op jit(solution)/shard_map/all_to_all | solution.py:94
  26.5 191.2 %all-to-all-start.2 = ((bf16[32,6,8192]{2,1,0:T(8,128)(2,1)}), bf16[32,6,8192]{2,1,0:T(8,128)(2,1)}, u32[]{:S(2)}, u32[]{:S(2)}) async-start(bf16[32,6,8192]{2,1,0:T(8,128)(2,1)} %reshape.110), calls=%async_computation.2 | async-start | bytes 8388608 | tf_op jit(solution)/shard_map/all_to_all | solution.py:87
  222.7 4.2 copy-start.3
  228.3 32.6 %all-to-all-start.5 = ((bf16[32,6,1024]{2,1,0:T(8,128)(2,1)}), bf16[32,6,1024]{2,1,0:T(8,128)(2,1)S(1)}, u32[]{:S(2)}, u32[]{:S(2)}) async-start(bf16[32,6,1024]{2,1,0:T(8,128)(2,1)} %reshape.114), calls=%async_computation.5 | async-start | bytes 1048576 | tf_op jit(solution)/shard_map/all_to_all | solution.py:112
  242.5 66.8 %copy-start.5 = (bf16[8192,128]{1,0:T(8,128)(2,1)S(1)}, bf16[8192,128]{1,0:T(8,128)(2,1)}, u32[]{:S(2)}) copy-start(bf16[8192,128]{1,0:T(8,128)(2,1)} %param.12) | copy-start | bytes 6291460
  260.9 105.2 %all-to-all-start.3 = ((bf16[32,6,8192]{2,1,0:T(8,128)(2,1)}), bf16[32,6,8192]{2,1,0:T(8,128)(2,1)}, u32[]{:S(2)}, u32[]{:S(2)}) async-start(bf16[32,6,8192]{2,1,0:T(8,128)(2,1)} %reshape.112), calls=%async_computation.3 | async-start | bytes 8388608 | tf_op jit(solution)/shard_map/all_to_all | solution.py:105
  366.0 26.8 %all-to-all-start.4 = ((bf16[8,96,128]{2,1,0:T(8,128)(2,1)}), bf16[8,96,128]{2,1,0:T(8,128)(2,1)S(1)}, u32[]{:S(2)}, u32[]{:S(2)}) async-start(bf16[8,96,128]{2,1,0:T(8,128)(2,1)} %bitcast.11), calls=%async_computation.4 | async-start | bytes 393216 | tf_op jit(solution)/shard_map/all_to_all | solution.py:64
  392.9 5.6 %copy-start.4 = (s32[96,1]{0,1:T(1,128)S(1)}, s32[96,1]{0,1:T(1,128)}, u32[]{:S(2)}) copy-start(s32[96,1]{0,1:T(1,128)} %param.9) | copy-start | bytes 1156
  392.9 40.0 %all-to-all-start = ((bf16[8,96,1024]{2,1,0:T(8,128)(2,1)}), bf16[8,96,1024]{2,1,0:T(8,128)(2,1)}, u32[]{:S(2)}, u32[]{:S(2)}) async-start(bf16[8,96,1024]{2,1,0:T(8,128)(2,1)} %bitcast), calls=%async_computation | async-start | bytes 3145728 | tf_op jit(solution)/shard_map/all_to_all | solution.py:63
  434.7 1.4 copy-start.2
  435.1 2.6 copy-start.1
Sparse Core Ops, SparseCore 0:
  10.2 299.0 all-gather.1
where the time goes:
time: 450 us; the launch traced here: 445 us
  waiting for transfers between devices  320 us (71%)
  starting transfers between devices  39.9 us (9%)
  matrix products  39 us (9%)
  local copies, waits for them, and re-layouts  25.2 us (6%)
  between operations  14.2 us (3%)
  other arithmetic  5.96 us (1%)
    all_to_all x1, waiting for transfers between devices, on_device(): lax.all_to_all(send_rows.reshape(devices, capacity, width), ('grp', 'tp')...  185 us
    all_to_all x1, waiting for transfers between devices, on_device(): lax.all_to_all(query_correction.reshape(lead, items, query_correction.sha...  49.6 us
    all_gather x1, waiting for transfers between devices, on_device(): piece = lax.all_gather(tokens, 'tp', axis=0, tiled=True)  40 us
    all_to_all x1, waiting for transfers between devices, on_device(): lax.all_to_all(projected[:, :query_cols], 'tp', split_axis=0, concat_axis...  26.5 us
    dot_general x1, matrix products, on_device(): jnp.dot(piece, query_base_output, preferred_element_type=jnp.float32)  19.9 us
    all_to_all x1, waiting for transfers between devices, on_device(): lax.all_to_all(value_correction.reshape(lead, items, value_correction.sha...  18.3 us
  transfers between devices with their start and end apart: 7, of which 5 were waited for; matrix products, arithmetic and copies ran while one was open for 15% of the time, Pallas kernels for 0%

commit v1 on v0

v1 whole, which is shorter than its diff:
```python
import jax
import jax.numpy as jnp
from jax import lax
from jax.sharding import PartitionSpec as P

adapter_scale = 2.0
F32 = jnp.float32
BF16 = jnp.bfloat16


def up_term(low, tenant, up):
    count, rank, cols = up.shape
    ids = jnp.arange(count, dtype=jnp.int32)
    flat = up.reshape(count * rank, cols)

    def rows_of(part):
        rows_low, rows_tenant = part
        wide = jnp.where(
            (rows_tenant[:, None] == ids[None, :])[:, :, None], rows_low[:, None, :], jnp.zeros((), BF16)
        )
        return jnp.dot(wide.reshape(rows_low.shape[0], count * rank), flat, preferred_element_type=F32)

    rows = low.shape[0]
    pieces = max(1, (rows * count * rank) // (1 << 22))
    if pieces == 1:
        return rows_of((low, tenant))
    out = lax.map(rows_of, (low.reshape(pieces, rows // pieces, rank), tenant.reshape(pieces, rows // pieces)))
    return out.reshape(rows, cols)


def on_device(tokens, holder, choice, wq, wv, down, up_q, up_v):
    members = lax.axis_size("tp")
    groups = lax.axis_size("grp")
    each = down.shape[0]
    rank = up_q.shape[1]
    tenant = (holder[:, 0] * each + choice[:, 0]).astype(jnp.int32)
    tenant = lax.all_gather(tenant, "tp", axis=0, tiled=True)
    piece = lax.all_gather(tokens, "tp", axis=0, tiled=True)
    downs = lax.all_gather(down, "grp", axis=0, tiled=True)
    all_q = lax.all_to_all(up_q, "tp", split_axis=2, concat_axis=0, tiled=True)
    all_v = lax.all_to_all(up_v, "tp", split_axis=2, concat_axis=0, tiled=True)
    all_q = lax.all_gather(all_q, "grp", axis=0, tiled=True)
    all_v = lax.all_gather(all_v, "grp", axis=0, tiled=True)

    slot = jnp.arange(groups * each, dtype=jnp.int32)
    here = ((slot // each) * members + lax.axis_index("tp")) * each + slot % each
    low = jnp.zeros((piece.shape[0], down.shape[2]), F32)
    for a in range(groups * each):
        part = jnp.dot(piece, downs[a], preferred_element_type=F32)
        low = low + jnp.where((tenant == here[a])[:, None], part, 0.0)
    low = lax.psum(low.astype(BF16), "tp")
    low = (adapter_scale * low).astype(BF16)

    base_q = jnp.dot(piece, wq, preferred_element_type=F32)
    base_v = jnp.dot(piece, wv, preferred_element_type=F32)
    out_q = (base_q + up_term(low[:, :rank], tenant, all_q)).astype(BF16)
    out_v = (base_v + up_term(low[:, rank:], tenant, all_v)).astype(BF16)
    queries = lax.all_to_all(out_q, "tp", split_axis=0, concat_axis=1, tiled=True)
    values = lax.all_to_all(out_v, "tp", split_axis=0, concat_axis=1, tiled=True)
    return queries, values


def solution(mesh):
    rows = P(("grp", "tp"), None)
    blocks = P(("grp", "tp"), None, None)
    return jax.shard_map(
        on_device,
        mesh=mesh,
        in_specs=(rows, rows, rows, P(None, "tp"), P(None, "tp"), blocks, blocks, blocks),
        out_specs=(rows, rows),
        check_vma=False,
    )
```

time: 450 us -> 594 us (1.32)
  waiting for transfers between devices: 320 us -> 401 us
  matrix products: 39 us -> 88.2 us
  local copies, waits for them, and re-layouts: 25.2 us -> 46.8 us
  starting transfers between devices: 39.9 us -> 22.3 us
  blocking collectives: 0 us -> 9.1 us
    all_to_all x6 -> x4, waiting for transfers between devices: 280 us -> 63.2 us  [the longest x1 33.8 us: on_device(): lax.all_to_all(out_q, 'tp', split_axis=0, concat_axis=1, tiled=True)]
    all_gather x0 -> x3, waiting for transfers between devices: none -> 179 us  [the longest x1 109 us: on_device(): downs = lax.all_gather(down, 'grp', axis=0, tiled=True)]
    all_gather x1, waiting for transfers between devices: 40 us -> 135 us  [on_device(): piece = lax.all_gather(tokens, 'tp', axis=0, tiled=True)]
    dot_general x7 -> x12, matrix products: 39 us -> 88.2 us  [the longest x8 48.5 us: on_device(): part = jnp.dot(piece, downs[a], preferred_element_type=F32)]
    unnamed x12 -> x24, local copies, waits for them, and re-layouts: 1.05 us -> 30.7 us
    psum x0 -> x1, waiting for transfers between devices: none -> 21.5 us  [on_device(): low = lax.psum(low.astype(BF16), 'tp')]
    reshape x6 -> x0, local copies, waits for them, and re-layouts: 19.4 us -> none  [the longest x1 5.03 us: on_device(): got_rows.reshape(lead * items, width)]
    all_to_all x6 -> x4, starting transfers between devices: 39.9 us -> 22.1 us  [the longest x1 5.66 us: on_device(): all_v = lax.all_to_all(up_v, 'tp', split_axis=2, concat_axis=0, tiled=True)]
  transfers between devices with their start and end apart: 7 -> 9, of which waited for: 5 -> 7; matrix products, arithmetic and copies ran while one was open for 15% -> 23% of each run, Pallas kernels for 0% -> 0%
where the time goes in v1:
time: 594 us; the launch traced here: 588 us
  waiting for transfers between devices  401 us (68%)
  matrix products  88.2 us (15%)
  local copies, waits for them, and re-layouts  46.8 us (8%)
  starting transfers between devices  22.3 us (4%)
  between operations  14.6 us (2%)
  blocking collectives  9.1 us (2%)
  other arithmetic  6.01 us (1%)
    all_gather x1, waiting for transfers between devices, on_device(): piece = lax.all_gather(tokens, 'tp', axis=0, tiled=True)  135 us
    all_gather x1, waiting for transfers between devices, on_device(): downs = lax.all_gather(down, 'grp', axis=0, tiled=True)  109 us
    all_gather x1, waiting for transfers between devices, on_device(): all_q = lax.all_gather(all_q, 'grp', axis=0, tiled=True)  50.5 us
    dot_general x8, matrix products, on_device(): part = jnp.dot(piece, downs[a], preferred_element_type=F32)  48.5 us
    all_to_all x1, waiting for transfers between devices, on_device(): lax.all_to_all(out_q, 'tp', split_axis=0, concat_axis=1, tiled=True)  33.8 us
    unnamed x24, local copies, waits for them, and re-layouts  30.7 us
    all_to_all x1, waiting for transfers between devices, on_device(): all_q = lax.all_to_all(up_q, 'tp', split_axis=2, concat_axis=0, tiled=True)  29.5 us
    psum x1, waiting for transfers between devices, on_device(): low = lax.psum(low.astype(BF16), 'tp')  21.5 us
  transfers between devices with their start and end apart: 9, of which 7 were waited for; matrix products, arithmetic and copies ran while one was open for 23% of the time, Pallas kernels for 0%

profile of v1, /device:TPU:13, one launch (start us, length us, event | category | flops | bytes accessed | tf_op | source)
XLA Modules:
  0.0 587.9 jit_solution(2526924030178083284)
XLA Ops:
  7.2 0.0 copy-start
  7.2 0.0 copy-start.6
  7.2 0.0 copy-start.2
  7.2 0.0 copy-start.3
  7.2 0.0 all-gather.6.cloned.1.call-start
  7.3 0.7 all-gather.6.cloned.1.call-update
  7.9 0.0 all-gather.8.cloned.1.call-start
  8.0 0.7 all-gather.8.cloned.1.call-update
  8.7 1.3 copy.21
  10.0 1.1 reshape.59
  11.1 5.7 all-to-all-start.2
  16.7 9.6 %copy.17 = bf16[2,64,8192]{1,0,2:T(2,128)(2,1)} copy(bf16[2,64,8192]{2,1,0:T(8,128)(2,1)} %param.14) | data formatting | bytes 4194304 | tf_op args[6]
  26.4 7.6 %reshape.57 = bf16[8,2,65536]{2,1,0:T(2,128)(2,1)} reshape(bf16[8192,2,64]{2,1,0:T(2,128)(2,1)} %bitcast.115) | data formatting | bytes 4194304
  34.0 0.0 copy-done.6
  34.0 0.6 dynamic-slice
  35.2 0.0 copy-done.2
  35.2 0.0 copy-done.3
  35.2 0.1 bitcast_dynamic-update-slice_fusion
  35.3 9.1 %all-reduce = s32[768]{0:T(1024)S(1)} all-reduce(s32[768]{0:T(1024)S(1)} %bitcast_dynamic-update-slice_fusion), channel_id=2, replica_groups=mesh['grp'=4,'tp'=8] {'tp'}, use_global_device_ids=true, to_apply=%add | all-reduce | flops 768 | bytes 6144 | tf_op jit(solution)/shard_map/all_gather | solution.py:37
  44.5 0.7 fusion.51
  45.1 4.9 broadcast_compare_fusion.7
  50.0 135.4 %all-gather.6.cloned.1.call-done = bf16[768,8192]{1,0:T(8,128)(2,1)} async-done(((bf16[96,8192]{1,0:T(8,128)(2,1)}), bf16[768,8192]{1,0:T(8,128)(2,1)}) %all-gather.6.cloned.1.call-update) | async-done | bytes 12582928 | tf_op jit(solution)/shard_map/all_gather | solution.py:38
  185.4 109.4 %all-gather.8.cloned.1.call-done = bf16[8,8192,128]{2,1,0:T(8,128)(2,1)} async-done(((bf16[2,8192,128]{2,1,0:T(8,128)(2,1)}), bf16[8,8192,128]{2,1,0:T(8,128)(2,1)}) %all-gather.8.cloned.1.call-update) | async-done | bytes 16777232 | tf_op jit(solution)/shard_map/all_gather | solution.py:39
  294.8 7.2 %fusion.37 = f32[768,128]{1,0:T(8,128)S(1)} fusion(bf16[768,8192]{1,0:T(8,128)(2,1)} %all-gather.6.cloned.1.call-done, bf16[8,8192,128]{2,1,0:T(8,128)(2,1)} %all-gather.8.cloned.1.call-done, pred[768]{0:T(1024)(128)(4,1)S(1)} %get-tuple-element.9), kind=kOutput, calls=%fused_computation.40 | convolution fusion | flops 1610711040 | bytes 15074048 | tf_op jit(solution)/shard_map/dot_general | solution.py:49
  302.0 0.0 copy-start.5
  302.0 2.8 copy-done.4
  304.8 7.9 %fusion.38 = f32[768,128]{1,0:T(8,128)S(1)} fusion(bf16[768,8192]{1,0:T(8,128)(2,1)} %all-gather.6.cloned.1.call-done, bf16[8,8192,128]{2,1,0:T(8,128)(2,1)S(1)} %copy-done.4, pred[768]{0:T(1024)(128)(4,1)S(1)} %get-tuple-element.8), kind=kOutput, calls=%fused_computation.41 | convolution fusion | flops 1610711040 | bytes 15074304 | tf_op jit(solution)/shard_map/dot_general | solution.py:49
  312.7 4.2 fusion.39
  316.8 4.2 fusion.40
  321.0 4.2 fusion.41
  325.1 4.1 fusion.42
  329.3 0.0 all-to-all-done.2
  329.3 5.5 all-to-all-start
  334.8 7.3 %fusion.43 = f32[768,128]{1,0:T(8,128)S(1)} fusion(bf16[768,8192]{1,0:T(8,128)(2,1)} %all-gather.6.cloned.1.call-done, bf16[8,8192,128]{2,1,0:T(8,128)(2,1)} %all-gather.8.cloned.1.call-done, pred[768]{0:T(1024)(128)(4,1)S(1)} %get-tuple-element.10), kind=kOutput, calls=%fused_computation.46 | convolution fusion | flops 1610711040 | bytes 15074048 | tf_op jit(solution)/shard_map/dot_general | solution.py:49
  342.1 9.6 %fusion.36 = bf16[768,128]{1,0:T(8,128)(2,1)} fusion(f32[768,128]{1,0:T(8,128)S(1)} %fusion.43, f32[768,128]{1,0:T(8,128)S(1)} %copy-done.7, f32[768,128]{1,0:T(8,128)} %fusion.41, f32[768,128]{1,0:T(8,128)} %fusion.40, f32[768,128]{1,0:T(8,128)} %fusion.39, f32[768,128]{1,0:T(8,128)S(1)} %fusion.38, f32[768,128]{1,0:T(8,128)S(1)} %fusion.37, ...), kind=kOutput, calls=%fused_computation.39 | convolution fusion | flops 1611497472 | bytes 17629952 | tf_op jit(solution)/shard_map/dot_general | solution.py:49
  351.6 0.0 all-reduce.3.cloned.1.call-update
  351.7 0.0 all-gather.12.cloned.1.call-start
  351.7 0.3 reshape.60
  352.1 1.0 copy.22
  353.1 0.0 all-gather.12.cloned.1.call-update
  353.1 0.0 all-gather.10.cloned.1.call-start
  353.1 29.5 %all-to-all-done = bf16[8,2,65536]{2,1,0:T(2,128)(2,1)} async-done(((bf16[8,2,65536]{2,1,0:T(2,128)(2,1)}), bf16[8,2,65536]{2,1,0:T(2,128)(2,1)}, u32[]{:S(2)}, u32[]{:S(2)}) %all-to-all-start) | async-done | bytes 2097184 | tf_op jit(solution)/shard_map/all_to_all | solution.py:40
  382.6 7.4 %reshape.58 = bf16[8192,2,64]{2,1,0:T(2,128)(2,1)} reshape(bf16[8,2,65536]{2,1,0:T(2,128)(2,1)} %all-to-all-done) | data formatting | bytes 4194304
  390.0 10.6 %copy.18 = bf16[8,2,64,1024]{3,2,1,0:T(8,128)(2,1)} copy(bf16[8,2,64,1024]{2,1,3,0:T(2,128)(2,1)} %bitcast.114) | data formatting | bytes 4194304 | tf_op jit(solution)/shard_map/all_to_all | solution.py:40
  400.6 0.0 all-gather.10.cloned.1.call-update
  400.7 6.4 %fusion.52 = f32[768,128]{1,0:T(8,128)S(1)} fusion(bf16[768,8192]{1,0:T(8,128)(2,1)} %all-gather.6.cloned.1.call-done, bf16[8192,128]{1,0:T(8,128)(2,1)S(1)} %copy-done), kind=kOutput, calls=%fused_computation.72 | convolution fusion | flops 1610612736 | bytes 15073280 | tf_op jit(solution)/shard_map/dot_general | solution.py:55
  407.1 21.5 %all-reduce.3.cloned.1.call-done = bf16[768,128]{1,0:T(8,128)(2,1)} async-done(((bf16[768,128]{1,0:T(8,128)(2,1)}), bf16[768,128]{1,0:T(8,128)(2,1)}) %all-reduce.3.cloned.1.call-update) | async-done | bytes 196624 | tf_op jit(solution)/shard_map/psum | solution.py:51
  428.6 0.9 broadcast_multiply_fusion
  429.6 0.1 fusion.50
  429.7 0.1 copy.16
  429.8 0.1 copy.20
  430.0 19.6 %all-gather.12.cloned.1.call-done = bf16[64,64,128]{2,1,0:T(8,128)(2,1)} async-done(((bf16[16,64,128]{2,1,0:T(8,128)(2,1)}), bf16[64,64,128]{2,1,0:T(8,128)(2,1)}) %all-gather.12.cloned.1.call-update) | async-done | bytes 1048592 | tf_op jit(solution)/shard_map/all_gather | solution.py:43
  449.6 3.8 fusion.25
  453.4 5.5 all-to-all-start.3
  458.8 50.5 %all-gather.10.cloned.1.call-done = bf16[64,64,1024]{2,1,0:T(8,128)(2,1)} async-done(((bf16[16,64,1024]{2,1,0:T(8,128)(2,1)}), bf16[64,64,1024]{2,1,0:T(8,128)(2,1)}) %all-gather.10.cloned.1.call-update) | async-done | bytes 8388624 | tf_op jit(solution)/shard_map/all_gather | solution.py:42
  509.3 9.1 %fusion.2 = f32[768,1024,1]{1,0,2:T(8,128)S(1)} fusion(bf16[64,64,1024]{2,1,0:T(8,128)(2,1)} %all-gather.10.cloned.1.call-done, pred[768,64]{0,1:T(8,128)(4,1)S(1)} %iota_compare_fusion, bf16[768,64]{0,1:T(8,128)(2,1)S(1)} %copy.16), kind=kOutput, calls=%fused_computation.2 | convolution fusion | flops 6445596672 | bytes 11681792 | tf_op jit(solution)/shard_map/dot_general | solution.py:21
  518.4 0.0 copy-start.1
  518.4 20.3 %fusion.6 = bf16[768,1024]{1,0:T(8,128)(2,1)} fusion(f32[768,1024,1]{1,0,2:T(8,128)S(1)} %fusion.2, bf16[768,8192]{1,0:T(8,128)(2,1)} %all-gather.6.cloned.1.call-done, bf16[8192,1024]{1,0:T(8,128)(2,1)} %param.11), kind=kOutput, calls=%fused_computation.7 | convolution fusion | flops 12886474752 | bytes 34078720 | tf_op jit(solution)/shard_map/dot_general | solution.py:54
  538.7 0.0 all-to-all-done.3
  538.7 5.5 all-to-all-start.1
  544.2 0.7 copy_bitcast_fusion
  544.9 33.8 %all-to-all-done.1 = bf16[8,96,1024]{2,1,0:T(8,128)(2,1)} async-done(((bf16[8,96,1024]{2,1,0:T(8,128)(2,1)}), bf16[8,96,1024]{2,1,0:T(8,128)(2,1)}, u32[]{:S(2)}, u32[]{:S(2)}) %all-to-all-start.1) | async-done | bytes 1572896 | tf_op jit(solution)/shard_map/all_to_all | solution.py:58
  578.7 2.7 copy.24
  581.4 0.0 copy-done.1
  (9 shorter events, 0.1 us)
Async XLA Ops:
  7.2 393.5 %copy-start = (bf16[8192,128]{1,0:T(8,128)(2,1)S(1)}, bf16[8192,128]{1,0:T(8,128)(2,1)}, u32[]{:S(2)}) copy-start(bf16[8192,128]{1,0:T(8,128)(2,1)} %param.12) | copy-start | bytes 6291460
  7.2 26.8 %copy-start.6 = (u32[32]{0:T(128)S(1)}, u32[32]{0:T(128)}, u32[]{:S(2)}) copy-start(u32[32]{0:T(128)} %constant.48) | copy-start | bytes 388
  7.2 28.0 %copy-start.2 = (s32[96,1]{0,1:T(1,128)S(1)}, s32[96,1]{0,1:T(1,128)}, u32[]{:S(2)}) copy-start(s32[96,1]{0,1:T(1,128)} %param.10) | copy-start | bytes 1156
  7.2 28.0 %copy-start.3 = (s32[96,1]{0,1:T(1,128)S(1)}, s32[96,1]{0,1:T(1,128)}, u32[]{:S(2)}) copy-start(s32[96,1]{0,1:T(1,128)} %param.9) | copy-start | bytes 1156
  7.2 178.2 %all-gather.6.cloned.1.call-start = ((), (), s32[]{:S(2)}) async-start(), calls=%async_computation.4 | async-start | bytes 14155776 | tf_op jit(solution)/shard_map/all_gather | solution.py:38
  7.9 286.8 %all-gather.8.cloned.1.call-start = ((), (), s32[]{:S(2)}) async-start(), calls=%async_computation.5 | async-start | bytes 20971520 | tf_op jit(solution)/shard_map/all_gather | solution.py:39
  11.1 318.2 %all-to-all-start.2 = ((bf16[8,2,8192]{2,1,0:T(2,128)(2,1)}), bf16[8,2,8192]{2,1,0:T(2,128)(2,1)S(1)}, u32[]{:S(2)}, u32[]{:S(2)}) async-start(bf16[8,2,8192]{2,1,0:T(2,128)(2,1)} %reshape.59), calls=%async_computation.2 | async-start | bytes 524288 | tf_op jit(solution)/shard_map/all_to_all | solution.py:41
  294.8 10.0 %copy-start.4 = (bf16[8,8192,128]{2,1,0:T(8,128)(2,1)S(1)}, bf16[8,8192,128]{2,1,0:T(8,128)(2,1)}, u32[]{:S(2)}) copy-start(bf16[8,8192,128]{2,1,0:T(8,128)(2,1)} %all-gather.8.cloned.1.call-done) | copy-start | bytes 50331652
  302.0 10.7 %copy-start.5 = (bf16[768,8192]{1,0:T(8,128)(2,1)S(1)}, bf16[768,8192]{1,0:T(8,128)(2,1)}, u32[]{:S(2)}) copy-start(bf16[768,8192]{1,0:T(8,128)(2,1)} %all-gather.6.cloned.1.call-done) | copy-start | bytes 37748740
  329.3 53.3 %all-to-all-start = ((bf16[8,2,65536]{2,1,0:T(2,128)(2,1)}), bf16[8,2,65536]{2,1,0:T(2,128)(2,1)}, u32[]{:S(2)}, u32[]{:S(2)}) async-start(bf16[8,2,65536]{2,1,0:T(2,128)(2,1)} %reshape.57), calls=%async_computation | async-start | bytes 4194304 | tf_op jit(solution)/shard_map/all_to_all | solution.py:40
  334.8 93.9 %all-reduce.3.cloned.1.call-start = ((), (), s32[]{:S(2)}) async-start(), calls=%async_computation.6 | async-start | bytes 393216 | tf_op jit(solution)/shard_map/psum | solution.py:51
  334.8 7.3 %copy-start.7 = (f32[768,128]{1,0:T(8,128)S(1)}, f32[768,128]{1,0:T(8,128)}, u32[]{:S(2)}) copy-start(f32[768,128]{1,0:T(8,128)} %fusion.42) | copy-start | bytes 1179652
  351.7 97.9 %all-gather.12.cloned.1.call-start = ((), (), s32[]{:S(2)}) async-start(), calls=%async_computation.8 | async-start | bytes 1310720 | tf_op jit(solution)/shard_map/all_gather | solution.py:43
  353.1 156.2 %all-gather.10.cloned.1.call-start = ((), (), s32[]{:S(2)}) async-start(), calls=%async_computation.7 | async-start | bytes 10485760 | tf_op jit(solution)/shard_map/all_gather | solution.py:42
  453.4 85.4 %all-to-all-start.3 = ((bf16[8,96,128]{2,1,0:T(8,128)(2,1)}), bf16[8,96,128]{2,1,0:T(8,128)(2,1)S(1)}, u32[]{:S(2)}, u32[]{:S(2)}) async-start(bf16[8,96,128]{2,1,0:T(8,128)(2,1)} %bitcast.28), calls=%async_computation.3 | async-start | bytes 393216 | tf_op jit(solution)/shard_map/all_to_all | solution.py:59
  518.4 63.0 %copy-start.1 = (bf16[8192,128]{1,0:T(8,128)(2,1)S(1)}, bf16[8192,128]{1,0:T(8,128)(2,1)}, u32[]{:S(2)}) copy-start(bf16[8192,128]{1,0:T(8,128)(2,1)} %param.12) | copy-start | bytes 6291460
  538.7 40.0 %all-to-all-start.1 = ((bf16[8,96,1024]{2,1,0:T(8,128)(2,1)}), bf16[8,96,1024]{2,1,0:T(8,128)(2,1)}, u32[]{:S(2)}, u32[]{:S(2)}) async-start(bf16[8,96,1024]{2,1,0:T(8,128)(2,1)} %bitcast.119), calls=%async_computation.1 | async-start | bytes 3145728 | tf_op jit(solution)/shard_map/all_to_all | solution.py:58
Sparse Core Ops, SparseCore 0:
  10.2 175.1 all-gather.5
  187.0 107.7 all-gather.7
  351.8 76.7 all-reduce.2
  430.6 18.9 all-gather.11
  451.0 58.2 all-gather.9

commit v2 on v1

v2 whole, which is shorter than its diff:
```python
import functools

import jax
import jax.numpy as jnp
from jax import lax
from jax.experimental import pallas as pl
from jax.experimental.pallas import tpu as pltpu
from jax.sharding import PartitionSpec as P

adapter_scale = 2.0
F32 = jnp.float32
BF16 = jnp.bfloat16
MESH = pl.DeviceIdType.MESH


def factor(n):
    first = 1
    while first * first < n:
        first *= 2
    return first, n // first


class Chain:
    def __init__(self, n1, n2, a, b, place, own, send, recv, device):
        self.n1, self.n2, self.a, self.b = n1, n2, a, b
        self.place, self.own, self.send, self.recv, self.device = place, own, send, recv, device

    def copy(self, block, s, t, way, to_a, to_b):
        return pltpu.make_async_remote_copy(
            src_ref=block,
            dst_ref=self.place(s, t),
            send_sem=self.send.at[s, t, way],
            recv_sem=self.recv.at[s, t],
            device_id=self.device(to_a, to_b),
            device_id_type=MESH,
        )

    def ways(self, s, t):
        a, b = self.a, self.b
        in_line = t == b
        return (
            (in_line & (s <= a) & (a + 1 < self.n1), 0, a + 1, b),
            (in_line & (s >= a) & (a >= 1), 1, a - 1, b),
            ((t <= b) & (b + 1 < self.n2), 2, a, b + 1),
            ((t >= b) & (b >= 1), 3, a, b - 1),
        )

    def each(self, s, t, act, own):
        block = self.own if own else self.place(s, t)
        for cond, way, to_a, to_b in self.ways(s, t):
            if self.n2 == 1 and way >= 2:
                continue

            @pl.when(cond)
            def _(way=way, to_a=to_a, to_b=to_b):
                act(self.copy(block, s, t, way, to_a, to_b))

    def begin(self):
        self.each(self.a, self.b, lambda c: c.start(), True)

    def arrive(self, s, t):
        self.copy(self.place(s, t), s, t, 0, self.a, self.b).wait_recv()
        self.each(s, t, lambda c: c.start(), False)

    def first_step(self, d):
        for s, ok in ((self.a - d, self.a >= d), (self.a + d, self.a + d < self.n1)):

            @pl.when(ok)
            def _(s=s):
                self.arrive(s, self.b)

    def second_step(self, d, e):
        sides = ((self.a, None),) if d == 0 else ((self.a - d, self.a >= d), (self.a + d, self.a + d < self.n1))
        for s, ok in sides:
            for t, ok2 in ((self.b - e, self.b >= e), (self.b + e, self.b + e < self.n2)):

                @pl.when(ok2 if ok is None else ok & ok2)
                def _(s=s, t=t):
                    self.arrive(s, t)

    def finish_second(self):
        for d in range(self.n1):
            for e in range(1, self.n2):
                self.second_step(d, e)

    def drain(self):
        def body(i, carry):
            s, t = i // self.n2, i % self.n2
            self.each(s, t, lambda c: c.wait_send(), False)
            return carry

        lax.fori_loop(0, self.n1 * self.n2, body, 0)


def exchange(
    sizes, tok, ten, down, upq, upv,
    tok_all, ten_all, down_all, upq_all, upv_all,
    tok_buf, ten_buf, down_buf, upq_buf, upv_buf,
    big_s, big_r, small_s, small_r, down_s, down_r, q_s, q_r, v_s, v_r,
    pq_s, pq_r, pv_s, pv_r, pt_s, pt_r, local_in, local_out,
):
    groups, members = sizes
    n1, n2 = factor(members)
    nx, nc = groups // 2, 2
    grp, tp = lax.axis_index("grp"), lax.axis_index("tp")
    a, b = tp // n2, tp % n2
    gx, gc = grp // nc, grp % nc
    rows = tok.shape[0]
    cols_q = upq.shape[2] // members
    cut = (rows // (members - 2) // 16 * 16) or 16

    barrier = pltpu.get_barrier_semaphore()
    for i in range(1, members):
        pl.semaphore_signal(barrier, inc=1, device_id=(grp, lax.rem(tp + i, members)), device_id_type=MESH)
    for i in range(1, groups):
        pl.semaphore_signal(barrier, inc=1, device_id=(lax.rem(grp + i, groups), tp), device_id_type=MESH)
    pl.semaphore_wait(barrier, members + groups - 2)

    def at_tp(first, second):
        return (grp, first * n2 + second)

    def at_tp_swapped(second, first):
        return (grp, first * n2 + second)

    def at_grp(first, second):
        return (first * nc + second, tp)

    big = Chain(
        n1, n2, a, b, lambda s, t: tok_all.at[s * n2 + t, pl.ds(cut, rows - cut)],
        tok.at[pl.ds(cut, rows - cut)], big_s, big_r, at_tp,
    )
    small = Chain(
        n2, n1, b, a, lambda t, s: tok_all.at[s * n2 + t, pl.ds(0, cut)],
        tok.at[pl.ds(0, cut)], small_s, small_r, at_tp_swapped,
    )
    downs = Chain(nx, nc, gx, gc, lambda s, t: down_all.at[s * nc + t], down, down_s, down_r, at_grp)
    ups_q = Chain(
        nx, nc, gx, gc, lambda s, t: upq_all.at[s * nc + t], upq_all.at[grp], q_s, q_r, at_grp
    )
    ups_v = Chain(
        nx, nc, gx, gc, lambda s, t: upv_all.at[s * nc + t], upv_all.at[grp], v_s, v_r, at_grp
    )

    def columns(ref, width, j):
        return ref.at[:, :, pl.ds(pl.multiple_of(j * width, width), width)]

    def peers(j, src_tp):
        dev = (grp, j)
        return (
            pltpu.make_async_remote_copy(
                src_ref=columns(upq, cols_q, j), dst_ref=upq_all.at[grp, src_tp],
                send_sem=pq_s.at[j], recv_sem=pq_r.at[src_tp], device_id=dev, device_id_type=MESH),
            pltpu.make_async_remote_copy(
                src_ref=upv.at[j], dst_ref=upv_all.at[grp, src_tp],
                send_sem=pv_s.at[j], recv_sem=pv_r.at[src_tp], device_id=dev, device_id_type=MESH),
            pltpu.make_async_remote_copy(
                src_ref=ten, dst_ref=ten_all.at[src_tp],
                send_sem=pt_s.at[j], recv_sem=pt_r.at[src_tp], device_id=dev, device_id_type=MESH),
        )

    small.begin()
    big.begin()
    downs.begin()
    for i in range(1, members):
        for copy in peers(lax.rem(tp + i, members), tp):
            copy.start()

    moves = (
        (columns(upq, cols_q, tp), upq_buf, upq_all.at[grp, tp]),
        (upv.at[tp], upv_buf, upv_all.at[grp, tp]),
        (ten, ten_buf, ten_all.at[tp]),
        (tok, tok_buf, tok_all.at[tp]),
        (down, down_buf, down_all.at[grp]),
    )
    for i, (source, held, target) in enumerate(moves):
        pltpu.make_async_copy(source, held, local_in.at[i]).start()
    for i, (source, held, target) in enumerate(moves):
        pltpu.make_async_copy(source, held, local_in.at[i]).wait()
        pltpu.make_async_copy(held, target, local_out.at[i]).start()
    for i, (source, held, target) in enumerate(moves):
        pltpu.make_async_copy(held, target, local_out.at[i]).wait()

    for d in range(1, max(n1, n2) + 1):
        if d < n1:
            big.first_step(d)
        if d == 1:
            for e in range(1, n2):
                small.first_step(e)
            for i in range(1, members):
                src_tp = lax.rem(tp + i, members)
                for copy in peers(src_tp, src_tp):
                    copy.wait_recv()
            ups_q.begin()
            ups_v.begin()
        if 1 < d <= n1:
            for e in range(n2):
                small.second_step(e, d - 1)
    for chain in (downs, ups_q, ups_v):
        for d in range(1, nx):
            chain.first_step(d)
    big.finish_second()
    for chain in (downs, ups_q, ups_v):
        chain.finish_second()
    for chain in (big, small, downs, ups_q, ups_v):
        chain.drain()
    for i in range(1, members):
        for copy in peers(lax.rem(tp + i, members), tp):
            copy.wait_send()


def gather_all(tokens, tenant, down, up_q, up_v, groups, members):
    n1, n2 = factor(members)
    nx, nc = groups // 2, 2
    rows = tokens.shape[0]
    each, rank = up_q.shape[:2]
    cq, cv = up_q.shape[2] // members, up_v.shape[2] // members
    ten = jnp.broadcast_to(tenant[:, None], (rows, 128))
    up_v = up_v.reshape(each, rank, members, cv).transpose(2, 0, 1, 3)
    shape = jax.ShapeDtypeStruct
    dma = pltpu.SemaphoreType.DMA
    grid2 = (dma((nx, nc, 4)), dma((nx, nc)))
    return pl.pallas_call(
        functools.partial(exchange, (groups, members)),
        out_shape=(
            shape((members,) + tokens.shape, BF16),
            shape((members, rows, 128), jnp.int32),
            shape((groups,) + down.shape, BF16),
            shape((groups, members, each, rank, cq), BF16),
            shape((groups, members, each, rank, cv), BF16),
        ),
        in_specs=[pl.BlockSpec(memory_space=pl.ANY)] * 5,
        out_specs=(pl.BlockSpec(memory_space=pl.ANY),) * 5,
        scratch_shapes=[
            pltpu.VMEM(tokens.shape, BF16),
            pltpu.VMEM((rows, 128), jnp.int32),
            pltpu.VMEM(down.shape, BF16),
            pltpu.VMEM((each, rank, cq), BF16),
            pltpu.VMEM((each, rank, cv), BF16),
            dma((n1, n2, 4)), dma((n1, n2)),
            dma((n2, n1, 4)), dma((n2, n1)),
            *grid2, *grid2, *grid2,
            dma((members,)), dma((members,)), dma((members,)), dma((members,)), dma((members,)), dma((members,)),
            dma((5,)), dma((5,)),
        ],
        compiler_params=pltpu.CompilerParams(collective_id=0, has_side_effects=True),
    )(tokens, ten, down, up_q, up_v)


def down_kernel(members, tok, ten, down, out):
    step = pl.program_id(0)
    each = down.shape[1]

    @pl.when(step == 0)
    def _():
        out[...] = jnp.zeros_like(out)

    maps = jnp.concatenate([down[0, i] for i in range(each)], axis=1)
    part = jnp.dot(tok[...], maps, preferred_element_type=F32)
    width = down.shape[3]
    first = (step * members + lax.axis_index("tp")) * each
    for i in range(each):
        keep = ten[...] == first + i
        out[...] += jnp.where(keep, part[:, i * width:(i + 1) * width], 0.0).astype(out.dtype)


def down_project(tok, ten, down, members):
    total = tok.shape[0]
    groups = down.shape[0]
    return pl.pallas_call(
        functools.partial(down_kernel, members),
        grid=(groups,),
        out_shape=jax.ShapeDtypeStruct((total, down.shape[3]), BF16),
        in_specs=[
            pl.BlockSpec(tok.shape, lambda g: (0, 0), pipeline_mode=pl.Buffered(1)),
            pl.BlockSpec(ten.shape, lambda g: (0, 0)),
            pl.BlockSpec((1,) + down.shape[1:], lambda g: (g, 0, 0, 0)),
        ],
        out_specs=pl.BlockSpec((total, down.shape[3]), lambda g: (0, 0)),
        compiler_params=pltpu.CompilerParams(vmem_limit_bytes=60 << 20),
    )(tok, ten, down)


def up_term(low, tenant, up):
    count, rank, cols = up.shape
    ids = jnp.arange(count, dtype=jnp.int32)
    flat = up.reshape(count * rank, cols)

    def rows_of(part):
        rows_low, rows_tenant = part
        wide = jnp.where(
            (rows_tenant[:, None] == ids[None, :])[:, :, None], rows_low[:, None, :], jnp.zeros((), BF16)
        )
        return jnp.dot(wide.reshape(rows_low.shape[0], count * rank), flat, preferred_element_type=F32)

    rows = low.shape[0]
    pieces = max(1, (rows * count * rank) // (1 << 22))
    if pieces == 1:
        return rows_of((low, tenant))
    out = lax.map(rows_of, (low.reshape(pieces, rows // pieces, rank), tenant.reshape(pieces, rows // pieces)))
    return out.reshape(rows, cols)


def on_device(tokens, holder, choice, wq, wv, down, up_q, up_v):
    members = lax.axis_size("tp")
    groups = lax.axis_size("grp")
    each, rank, _ = up_q.shape
    mine = (holder[:, 0] * each + choice[:, 0]).astype(jnp.int32)
    tok, ten, downs, all_q, all_v = gather_all(tokens, mine, down, up_q, up_v, groups, members)
    total = members * tokens.shape[0]
    tok = tok.reshape(total, tokens.shape[1])
    ten = ten.reshape(total, 128)
    tenant = ten[:, 0]
    low = down_project(tok, ten, downs, members)
    low = lax.psum(low, "tp")
    low = (adapter_scale * low).astype(BF16)
    base_q = jnp.dot(tok, wq, preferred_element_type=F32)
    base_v = jnp.dot(tok, wv, preferred_element_type=F32)
    count = groups * members * each
    out_q = (base_q + up_term(low[:, :rank], tenant, all_q.reshape(count, rank, -1))).astype(BF16)
    out_v = (base_v + up_term(low[:, rank:], tenant, all_v.reshape(count, rank, -1))).astype(BF16)
    queries = lax.all_to_all(out_q, "tp", split_axis=0, concat_axis=1, tiled=True)
    values = lax.all_to_all(out_v, "tp", split_axis=0, concat_axis=1, tiled=True)
    return queries, values


def solution(mesh):
    rows = P(("grp", "tp"), None)
    blocks = P(("grp", "tp"), None, None)
    return jax.shard_map(
        on_device,
        mesh=mesh,
        in_specs=(rows, rows, rows, P(None, "tp"), P(None, "tp"), blocks, blocks, blocks),
        out_specs=(rows, rows),
        check_vma=False,
    )
```

time: 594 us -> 386 us (0.65)
  waiting for transfers between devices: 401 us -> 108 us
  Pallas kernels: 0 us -> 197 us
  matrix products: 88.2 us -> 40.2 us
  local copies, waits for them, and re-layouts: 46.8 us -> 6.54 us
  starting transfers between devices: 22.3 us -> 9.92 us
  blocking collectives: 9.1 us -> 0 us
    all_gather x4 -> x0, waiting for transfers between devices: 315 us -> none  [the longest x1 135 us: on_device(): piece = lax.all_gather(tokens, 'tp', axis=0, tiled=True)]
    pallas_call x0 -> x2, Pallas kernels: none -> 197 us  [the longest x1 176 us: gather_all(): pl.pallas_call(functools.partial(exchange, (groups, members)), out_shape=...]
    psum x1, waiting for transfers between devices: 21.5 us -> 74.5 us  [on_device(): low = lax.psum(low, 'tp')]
    dot_general x10 -> x2, matrix products: 75.3 us -> 26.7 us  [the longest x1 20.3 us: on_device(): base_q = jnp.dot(tok, wq, preferred_element_type=F32)]
    unnamed x24 -> x8, local copies, waits for them, and re-layouts: 30.7 us -> 0.03 us
    all_to_all x2 -> x0, waiting for transfers between devices: 29.5 us -> none  [the longest x1 29.5 us: on_device(): all_q = lax.all_to_all(up_q, 'tp', split_axis=2, concat_axis=0, tiled=True)]
    all_to_all x2 -> x0, local copies, waits for them, and re-layouts: 11.6 us -> none  [the longest x1 10.6 us: on_device(): all_q = lax.all_to_all(up_q, 'tp', split_axis=2, concat_axis=0, tiled=True)]
    all_to_all x2 -> x0, starting transfers between devices: 11.1 us -> none  [the longest x1 5.66 us: on_device(): all_v = lax.all_to_all(up_v, 'tp', split_axis=2, concat_axis=0, tiled=True)]
  transfers between devices with their start and end apart: 9 -> 3, of which waited for: 7 -> 2; matrix products, arithmetic and copies ran while one was open for 23% -> 10% of each run, Pallas kernels for 0% -> 0%
where the time goes in v2:
time: 386 us; the launch traced here: 381 us
  Pallas kernels  197 us (51%)
  waiting for transfers between devices  108 us (28%)
  matrix products  40.2 us (10%)
  between operations  14.1 us (4%)
  starting transfers between devices  9.92 us (3%)
  local copies, waits for them, and re-layouts  6.54 us (2%)
  other arithmetic  5.18 us (1%)
    pallas_call x1, Pallas kernels, gather_all(): pl.pallas_call(functools.partial(exchange, (groups, members)), out_shape=...  176 us
    psum x1, waiting for transfers between devices, on_device(): low = lax.psum(low, 'tp')  74.5 us
    all_to_all x1, waiting for transfers between devices, on_device(): lax.all_to_all(out_q, 'tp', split_axis=0, concat_axis=1, tiled=True)  33.8 us
    pallas_call x1, Pallas kernels, down_project(): pl.pallas_call(functools.partial(down_kernel, members), grid=(groups,), o...  20.6 us
    dot_general x1, matrix products, on_device(): base_q = jnp.dot(tok, wq, preferred_element_type=F32)  20.3 us
    dot_general x2, matrix products, rows_of(): jnp.dot(wide.reshape(rows_low.shape[0], count * rank), flat, preferred_el...  13.5 us
  transfers between devices with their start and end apart: 3, of which 2 were waited for; matrix products, arithmetic and copies ran while one was open for 10% of the time, Pallas kernels for 0%

profile of v2, /device:TPU:13, one launch (start us, length us, event | category | flops | bytes accessed | tf_op | source)
XLA Modules:
  0.0 381.3 jit_solution(16942888651234486758)
XLA Ops:
  7.2 0.0 copy-start
  7.2 0.0 all-reduce.2.cloned.1.call-start
  7.2 1.9 bitcast_bitcast_fusion.upv
  9.1 0.7 add_bitcast_fusion
  9.8 0.7 broadcast_in_dim.44.ten
  10.5 176.4 %shard_map.95 = (bf16[8,96,8192]{2,1,0:T(8,128)(2,1)}, s32[8,96,128]{2,1,0:T(8,128)}, bf16[4,2,8192,128]{3,2,1,0:T(8,128)(2,1)}, bf16[4,8,2,64,1024]{4,3,2,1,0:T(8,128)(2,1)}, bf16[4,8,2,64,128]{4,3,2,1,0:T(8,128)(2,1)}) custom-call(bf16[96,8192]{1,0:T(8,128)(2,1)} %tok.1, s32[96,128]{1,0:T(8,128)} %broadcast_in_dim.44.ten, bf16[2,8192,128]{2,1,0:T(8,128)(2,1)} %down.1, ...), custom_call_target="tpu_custom_call" | custom-call | tf_op jit(solution)/shard_map/pallas_call | solution.py:222
  186.9 0.0 copy-start.2
  186.9 20.6 %shard_map.96 = bf16[768,128]{1,0:T(8,128)(2,1)} custom-call(bf16[768,8192]{1,0:T(8,128)(2,1)} %bitcast.34, s32[768,128]{1,0:T(8,128)} %bitcast.39, bf16[4,2,8192,128]{3,2,1,0:T(8,128)(2,1)} %get-tuple-element.9.down), custom_call_target="tpu_custom_call" | custom-call | tf_op jit(solution)/shard_map/pallas_call | solution.py:269
  207.5 0.0 all-reduce.2.cloned.1.call-update
  207.5 0.0 copy-done.2
  207.5 0.2 slice_reduce_fusion
  207.7 0.0 copy-done
  207.7 6.4 %fusion.3 = f32[768,128]{1,0:T(8,128)S(1)} fusion(bf16[768,8192]{1,0:T(8,128)(2,1)} %bitcast.35, bf16[8192,128]{1,0:T(8,128)(2,1)S(1)} %copy-done), kind=kOutput, calls=%fused_computation.13 | convolution fusion | flops 1610612736 | bytes 15073280 | tf_op jit(solution)/shard_map/dot_general | solution.py:317
  214.2 74.5 %all-reduce.2.cloned.1.call-done = bf16[768,128]{1,0:T(8,128)(2,1)} async-done(((bf16[768,128]{1,0:T(8,128)(2,1)}), bf16[768,128]{1,0:T(8,128)(2,1)}) %all-reduce.2.cloned.1.call-update) | async-done | bytes 196624 | tf_op jit(solution)/shard_map/psum | solution.py:314
  288.7 0.9 broadcast_multiply_fusion
  289.6 0.1 fusion.1
  289.8 0.1 copy.15
  289.9 0.1 copy.13
  290.0 0.0 copy-start.3
  290.0 3.5 broadcast_select_fusion
  293.6 0.0 copy-done.3
  293.6 2.6 fusion
  296.1 4.4 %all-to-all-start.1 = ((bf16[8,96,128]{2,1,0:T(8,128)(2,1)}), bf16[8,96,128]{2,1,0:T(8,128)(2,1)S(1)}, u32[]{:S(2)}, u32[]{:S(2)}) async-start(bf16[8,96,128]{2,1,0:T(8,128)(2,1)} %bitcast.10), calls=%async_computation.1 | async-start | bytes 393216 | tf_op jit(solution)/shard_map/all_to_all | solution.py:322
  300.6 11.0 %fusion.2 = f32[768,1024]{1,0:T(8,128)S(1)} fusion(bf16[768,4096]{0,1:T(8,128)(2,1)} %bitcast.37, bf16[4096,1024]{1,0:T(8,128)(2,1)} %bitcast.43), kind=kOutput, calls=%fused_computation.12 | convolution fusion | flops 6442450944 | bytes 17825792 | tf_op jit(solution)/shard_map/dot_general | solution.py:293
  311.5 0.0 copy-start.1
  311.5 20.3 %add_convert_fusion = bf16[768,1024]{1,0:T(8,128)(2,1)} fusion(f32[768,1024]{1,0:T(8,128)S(1)} %fusion.2, bf16[768,8192]{1,0:T(8,128)(2,1)} %bitcast.36, bf16[8192,1024]{1,0:T(8,128)(2,1)} %param.11), kind=kOutput, calls=%fused_computation.2 | convolution fusion | flops 12886474752 | bytes 34078720 | tf_op jit(solution)/shard_map/dot_general | solution.py:316
  331.8 0.0 all-to-all-done.1
  331.8 5.4 %all-to-all-start = ((bf16[8,96,1024]{2,1,0:T(8,128)(2,1)}), bf16[8,96,1024]{2,1,0:T(8,128)(2,1)}, u32[]{:S(2)}, u32[]{:S(2)}) async-start(bf16[8,96,1024]{2,1,0:T(8,128)(2,1)} %bitcast.41), calls=%async_computation | async-start | bytes 3145728 | tf_op jit(solution)/shard_map/all_to_all | solution.py:321
  337.3 0.7 copy_bitcast_fusion
  338.0 33.8 %all-to-all-done = bf16[8,96,1024]{2,1,0:T(8,128)(2,1)} async-done(((bf16[8,96,1024]{2,1,0:T(8,128)(2,1)}), bf16[8,96,1024]{2,1,0:T(8,128)(2,1)}, u32[]{:S(2)}, u32[]{:S(2)}) %all-to-all-start) | async-done | bytes 1572896 | tf_op jit(solution)/shard_map/all_to_all | solution.py:321
  371.7 2.7 copy.18
  374.5 0.0 copy-done.1
  (1 shorter events, 0.0 us)
Async XLA Ops:
  7.2 200.5 %copy-start = (bf16[8192,128]{1,0:T(8,128)(2,1)S(1)}, bf16[8192,128]{1,0:T(8,128)(2,1)}, u32[]{:S(2)}) copy-start(bf16[8192,128]{1,0:T(8,128)(2,1)} %param.12) | copy-start | bytes 6291460
  7.2 281.5 %all-reduce.2.cloned.1.call-start = ((), (), s32[]{:S(2)}) async-start(), calls=%async_computation.2 | async-start | bytes 393216 | tf_op jit(solution)/shard_map/psum | solution.py:314
  186.9 20.7 %copy-start.2 = (s32[8,96,128]{2,1,0:T(8,128)S(1)}, s32[8,96,128]{2,1,0:T(8,128)}, u32[]{:S(2)}) copy-start(s32[8,96,128]{2,1,0:T(8,128)} %get-tuple-element.8) | copy-start | bytes 1179652
  290.0 3.5 copy-start.3
  296.1 35.7 %all-to-all-start.1 = ((bf16[8,96,128]{2,1,0:T(8,128)(2,1)}), bf16[8,96,128]{2,1,0:T(8,128)(2,1)S(1)}, u32[]{:S(2)}, u32[]{:S(2)}) async-start(bf16[8,96,128]{2,1,0:T(8,128)(2,1)} %bitcast.10), calls=%async_computation.1 | async-start | bytes 393216 | tf_op jit(solution)/shard_map/all_to_all | solution.py:322
  311.5 62.9 %copy-start.1 = (bf16[8192,128]{1,0:T(8,128)(2,1)S(1)}, bf16[8192,128]{1,0:T(8,128)(2,1)}, u32[]{:S(2)}) copy-start(bf16[8192,128]{1,0:T(8,128)(2,1)} %param.12) | copy-start | bytes 6291460
  331.8 39.9 %all-to-all-start = ((bf16[8,96,1024]{2,1,0:T(8,128)(2,1)}), bf16[8,96,1024]{2,1,0:T(8,128)(2,1)}, u32[]{:S(2)}, u32[]{:S(2)}) async-start(bf16[8,96,1024]{2,1,0:T(8,128)(2,1)} %bitcast.41), calls=%async_computation | async-start | bytes 3145728 | tf_op jit(solution)/shard_map/all_to_all | solution.py:321
Sparse Core Ops, SparseCore 0:
  207.6 80.9 all-reduce.1

commit v3 on v2

--- a/solution.py
+++ b/solution.py
@@ -280,24 +280,156 @@
     )(tok, ten, down)
 
 
-def up_term(low, tenant, up):
-    count, rank, cols = up.shape
-    ids = jnp.arange(count, dtype=jnp.int32)
-    flat = up.reshape(count * rank, cols)
-
-    def rows_of(part):
-        rows_low, rows_tenant = part
-        wide = jnp.where(
-            (rows_tenant[:, None] == ids[None, :])[:, :, None], rows_low[:, None, :], jnp.zeros((), BF16)
-        )
-        return jnp.dot(wide.reshape(rows_low.shape[0], count * rank), flat, preferred_element_type=F32)
-
-    rows = low.shape[0]
-    pieces = max(1, (rows * count * rank) // (1 << 22))
-    if pieces == 1:
-        return rows_of((low, tenant))
-    out = lax.map(rows_of, (low.reshape(pieces, rows // pieces, rank), tenant.reshape(pieces, rows // pieces)))
-    return out.reshape(rows, cols)
+def finish_kernel(
+    members, rank, part, ten, base_q, base_v, upq, upv, out_q, out_v,
+    inbox, mine, low, wide, held_q, held_v,
+    s1, r1, s2, r2, sq, rq, sv, rv, loc,
+):
+    grp, me = lax.axis_index("grp"), lax.axis_index("tp")
+    rows = mine.shape[0]
+    width = mine.shape[1]
+    cols_q = base_q.shape[1]
+    pair = 2 * rows
+    pairs = members // 2
+
+    barrier = pltpu.get_barrier_semaphore()
+    for i in range(1, members):
+        pl.semaphore_signal(barrier, inc=1, device_id=(grp, lax.rem(me + i, members)), device_id_type=MESH)
+    pl.semaphore_wait(barrier, members - 1)
+
+    def remote(src, dst, send, recv, j):
+        return pltpu.make_async_remote_copy(
+            src_ref=src, dst_ref=dst, send_sem=send, recv_sem=recv, device_id=(grp, j), device_id_type=MESH
+        )
+
+    def collect(j, source):
+        return remote(part.at[j], inbox.at[source], s1.at[j], r1.at[source], j)
+
+    def spread(j, source):
+        return remote(mine, low.at[source], s2.at[j], r2.at[source], j)
+
+    own = pltpu.make_async_copy(part.at[me], inbox.at[me], loc.at[0])
+    own.start()
+    for i in range(1, members):
+        collect(lax.rem(me + i, members), me).start()
+    own.wait()
+    for i in range(1, members):
+        j = lax.rem(me + i, members)
+        collect(j, j).wait_recv()
+    total = inbox[0].astype(F32)
+    for i in range(1, members):
+        total = total + inbox[i].astype(F32)
+    mine[...] = (adapter_scale * total).astype(BF16)
+    for i in range(1, members):
+        collect(lax.rem(me + i, members), me).wait_send()
+    for i in range(1, members):
+        spread(lax.rem(me + i, members), me).start()
+    own = pltpu.make_async_copy(mine, low.at[me], loc.at[0])
+    own.start()
+    own.wait()
+    for i in range(1, members):
+        j = lax.rem(me + i, members)
+        spread(j, j).wait_recv()
+    for i in range(1, members):
+        spread(lax.rem(me + i, members), me).wait_send()
+
+    lane = lax.broadcasted_iota(jnp.int32, (pair, width), 1)
+    share = lane // rank
+    count = upq.shape[0] // rank
+
+    def home(j, source):
+        columns = pl.ds(pl.multiple_of(source * cols_q, cols_q), cols_q)
+        return (
+            remote(held_q.at[j], out_q.at[:, columns], sq.at[j], rq.at[source], j),
+            remote(held_v.at[j], out_v.at[source], sv.at[j], rv.at[source], j),
+        )
+
+    def kept():
+        columns = pl.ds(pl.multiple_of(me * cols_q, cols_q), cols_q)
+        return (
+            pltpu.make_async_copy(held_q.at[me], out_q.at[:, columns], loc.at[0]),
+            pltpu.make_async_copy(held_v.at[me], out_v.at[me], loc.at[1]),
+        )
+
+    def place(i):
+        return lax.rem(me // 2 + i + 1, pairs)
+
+    def send(i):
+        for k in range(2):
+            j = 2 * place(i) + k
+
+            @pl.when(j != me)
+            def _():
+                for copy in home(j, me):
+                    copy.start()
+
+            @pl.when(j == me)
+            def _():
+                for copy in kept():
+                    copy.start()
+
+    def body(i, carry):
+        p = place(i)
+        at = pl.ds(pl.multiple_of(p * pair, pair), pair)
+        tenant = ten[at, :]
+        value = low[pl.ds(2 * p, 2)].reshape(pair, width).astype(F32)
+        turned = pltpu.roll(value, rank, 1)
+        parts = (jnp.where(lane < rank, value, turned), jnp.where(lane < rank, turned, value))
+        for which, (base, up, held) in enumerate(((base_q, upq, held_q), (base_v, upv, held_v))):
+            for c in range(count // 2):
+                keep = tenant == share + 2 * c
+                wide[:, c * width:(c + 1) * width] = jnp.where(keep, parts[which], 0.0).astype(BF16)
+            result = base[at, :] + jnp.dot(wide[...], up[...], preferred_element_type=F32)
+            held[pl.ds(2 * p, 2)] = result.astype(BF16).reshape(2, rows, result.shape[1])
+
+        @pl.when(i > 0)
+        def _():
+            send(i - 1)
+
+        return carry
+
+    lax.fori_loop(0, pairs, body, 0)
+    send(pairs - 1)
+    for i in range(1, members):
+        j = lax.rem(me + i, members)
+        for copy in home(j, j):
+            copy.wait_recv()
+        for copy in home(j, me):
+            copy.wait_send()
+    for copy in kept():
+        copy.wait()
+
+
+def finish(part, ten, base_q, base_v, upq, upv, members, rank):
+    total, width = part.shape
+    rows = total // members
+    cq, cv = base_q.shape[1], base_v.shape[1]
+    dma = pltpu.SemaphoreType.DMA
+    whole = pl.BlockSpec(memory_space=pltpu.VMEM)
+    left = pl.BlockSpec(memory_space=pl.ANY)
+    queries, values = pl.pallas_call(
+        functools.partial(finish_kernel, members, rank),
+        out_shape=(
+            jax.ShapeDtypeStruct((rows, members * cq), BF16),
+            jax.ShapeDtypeStruct((members, rows, cv), BF16),
+        ),
+        in_specs=[left, whole, whole, whole, whole, whole],
+        out_specs=(left, left),
+        scratch_shapes=[
+            pltpu.VMEM((members, rows, width), BF16),
+            pltpu.VMEM((rows, width), BF16),
+            pltpu.VMEM((members, rows, width), BF16),
+            pltpu.VMEM((2 * rows, upq.shape[0]), BF16),
+            pltpu.VMEM((members, rows, cq), BF16),
+            pltpu.VMEM((members, rows, cv), BF16),
+            *[dma((members,))] * 8,
+            dma((2,)),
+        ],
+        compiler_params=pltpu.CompilerParams(
+            collective_id=1, has_side_effects=True, vmem_limit_bytes=58 << 20
+        ),
+    )(part.reshape(members, rows, width), ten, base_q, base_v, upq, upv)
+    return queries, values.transpose(1, 0, 2).reshape(rows, members * cv)
 
 
 def on_device(tokens, holder, choice, wq, wv, down, up_q, up_v):
@@ -309,17 +441,13 @@
     total = members * tokens.shape[0]
     tok = tok.reshape(total, tokens.shape[1])
     ten = ten.reshape(total, 128)
-    tenant = ten[:, 0]
     low = down_project(tok, ten, downs, members)
-    low = lax.psum(low, "tp")
-    low = (adapter_scale * low).astype(BF16)
     base_q = jnp.dot(tok, wq, preferred_element_type=F32)
     base_v = jnp.dot(tok, wv, preferred_element_type=F32)
-    count = groups * members * each
-    out_q = (base_q + up_term(low[:, :rank], tenant, all_q.reshape(count, rank, -1))).astype(BF16)
-    out_v = (base_v + up_term(low[:, rank:], tenant, all_v.reshape(count, rank, -1))).astype(BF16)
-    queries = lax.all_to_all(out_q, "tp", split_axis=0, concat_axis=1, tiled=True)
-    values = lax.all_to_all(out_v, "tp", split_axis=0, concat_axis=1, tiled=True)
+    depth = groups * members * each * rank
+    queries, values = finish(
+        low, ten, base_q, base_v, all_q.reshape(depth, -1), all_v.reshape(depth, -1), members, rank
+    )
     return queries, values
 
 

time: 386 us -> 311 us (0.81); the launches traced: 381 us -> 310 us
  waiting for transfers between devices: 108 us -> 0 us
  Pallas kernels: 197 us -> 277 us
  matrix products: 40.2 us -> 24.5 us
  between operations: 14.1 us -> 0.66 us
  starting transfers between devices: 9.92 us -> 0 us
  other arithmetic: 5.18 us -> 0.82 us
    pallas_call x0 -> x1, Pallas kernels: none -> 79.6 us  [finish(): pl.pallas_call(functools.partial(finish_kernel, members, rank), out_shape...]
    psum x1 -> x0, waiting for transfers between devices: 74.5 us -> none  [on_device(): low = lax.psum(low, 'tp')]
    all_to_all x2 -> x0, waiting for transfers between devices: 33.8 us -> none  [the longest x1 33.8 us: on_device(): lax.all_to_all(out_q, 'tp', split_axis=0, concat_axis=1, tiled=True)]
    dot_general x2 -> x0, matrix products: 13.5 us -> none  [rows_of(): jnp.dot(wide.reshape(rows_low.shape[0], count * rank), flat, preferred_el...]
    all_to_all x2 -> x0, starting transfers between devices: 9.88 us -> none  [the longest x1 5.44 us: on_device(): lax.all_to_all(out_q, 'tp', split_axis=0, concat_axis=1, tiled=True)]
  transfers between devices with their start and end apart: 3 -> 0, of which waited for: 2 -> 0; matrix products, arithmetic and copies ran while one was open for 10% -> 0% of each run, Pallas kernels for 0% -> 0%
where the time goes in v3:
time: 311 us; the launch traced here: 310 us
  Pallas kernels  277 us (89%)
  matrix products  24.5 us (8%)
  local copies, waits for them, and re-layouts  7.75 us (2%)
    pallas_call x1, Pallas kernels, gather_all(): pl.pallas_call(functools.partial(exchange, (groups, members)), out_shape=...  176 us
    pallas_call x1, Pallas kernels, finish(): pl.pallas_call(functools.partial(finish_kernel, members, rank), out_shape...  79.6 us
    pallas_call x1, Pallas kernels, down_project(): pl.pallas_call(functools.partial(down_kernel, members), grid=(groups,), o...  20.6 us
    dot_general x1, matrix products, on_device(): base_q = jnp.dot(tok, wq, preferred_element_type=F32)  17.2 us
    dot_general x1, matrix products, on_device(): base_v = jnp.dot(tok, wv, preferred_element_type=F32)  7.28 us

profile of v3, /device:TPU:13, one launch (start us, length us, event | category | flops | bytes accessed | tf_op | source)
XLA Modules:
  0.0 310.3 jit_solution(5065268394828948026)
XLA Ops:
  0.6 0.0 copy-start
  0.6 0.8 add_bitcast_fusion
  1.5 0.7 broadcast_in_dim.9.ten
  2.2 1.7 bitcast_bitcast_fusion.upv
  3.9 176.4 %shard_map.95 = (bf16[8,96,8192]{2,1,0:T(8,128)(2,1)}, s32[8,96,128]{2,1,0:T(8,128)}, bf16[4,2,8192,128]{3,2,1,0:T(8,128)(2,1)}, bf16[4,8,2,64,1024]{4,3,2,1,0:T(8,128)(2,1)}, bf16[4,8,2,64,128]{4,3,2,1,0:T(8,128)(2,1)}) custom-call(bf16[96,8192]{1,0:T(8,128)(2,1)} %tok.1, s32[96,128]{1,0:T(8,128)} %broadcast_in_dim.9.ten, bf16[2,8192,128]{2,1,0:T(8,128)(2,1)} %down.1, ...), custom_call_target="tpu_custom_call" | custom-call | tf_op jit(solution)/shard_map/pallas_call | solution.py:222
  180.3 20.6 %shard_map.96 = bf16[768,128]{1,0:T(8,128)(2,1)} custom-call(bf16[768,8192]{1,0:T(8,128)(2,1)} %bitcast.24, s32[768,128]{1,0:T(8,128)} %bitcast.28, bf16[4,2,8192,128]{3,2,1,0:T(8,128)(2,1)} %get-tuple-element.11.down), custom_call_target="tpu_custom_call" | custom-call | tf_op jit(solution)/shard_map/pallas_call | solution.py:269
  200.9 0.0 copy-start.2
  200.9 0.0 copy-done
  200.9 7.3 %fusion.1.base_v = f32[768,128]{1,0:T(8,128)} fusion(bf16[768,8192]{1,0:T(8,128)(2,1)} %bitcast.25, bf16[8192,128]{1,0:T(8,128)(2,1)S(1)} %copy-done), kind=kOutput, calls=%fused_computation.4 | convolution fusion | flops 1610612736 | bytes 15073280 | tf_op jit(solution)/shard_map/dot_general | solution.py:446
  208.2 1.0 copy-done.2
  209.2 0.0 copy-start.1
  209.2 17.2 %fusion.base_q = f32[768,1024]{1,0:T(8,128)} fusion(bf16[768,8192]{1,0:T(8,128)(2,1)S(1)} %bitcast.26, bf16[8192,1024]{1,0:T(8,128)(2,1)} %param.11), kind=kOutput, calls=%fused_computation.3 | convolution fusion | flops 12884901888 | bytes 32505856 | tf_op jit(solution)/shard_map/dot_general | solution.py:445
  226.4 79.6 %shard_map.97 = (bf16[96,8192]{1,0:T(8,128)(2,1)}, bf16[8,96,128]{2,1,0:T(8,128)(2,1)}) custom-call(bf16[8,96,128]{2,1,0:T(8,128)(2,1)} %bitcast.31, s32[768,128]{1,0:T(8,128)} %bitcast.29, f32[768,1024]{1,0:T(8,128)} %fusion.base_q, f32[768,128]{1,0:T(8,128)} %fusion.1.base_v, bf16[4096,1024]{1,0:T(8,128)(2,1)} %bitcast.27, bf16[4096,128]{1,0:T(8,128)(2,1)} %bitcast.30), custom_call_target="tpu_custom_call" | custom-call | tf_op jit(solution)/shard_map/pallas_call | solution.py:410
  306.0 1.6 copy_bitcast_fusion
  307.6 2.7 copy.17
  310.3 0.0 copy-done.1
Async XLA Ops:
  0.6 200.3 %copy-start = (bf16[8192,128]{1,0:T(8,128)(2,1)S(1)}, bf16[8192,128]{1,0:T(8,128)(2,1)}, u32[]{:S(2)}) copy-start(bf16[8192,128]{1,0:T(8,128)(2,1)} %param.12) | copy-start | bytes 6291460
  200.9 8.3 %copy-start.2 = (bf16[8,96,8192]{2,1,0:T(8,128)(2,1)S(1)}, bf16[8,96,8192]{2,1,0:T(8,128)(2,1)}, u32[]{:S(2)}) copy-start(bf16[8,96,8192]{2,1,0:T(8,128)(2,1)} %get-tuple-element.9) | copy-start | bytes 37748740
  209.2 101.1 %copy-start.1 = (bf16[8192,128]{1,0:T(8,128)(2,1)S(1)}, bf16[8192,128]{1,0:T(8,128)(2,1)}, u32[]{:S(2)}) copy-start(bf16[8192,128]{1,0:T(8,128)(2,1)} %param.12) | copy-start | bytes 6291460

commit v4 on v3

--- a/solution.py
+++ b/solution.py
@@ -96,7 +96,7 @@
     sizes, tok, ten, down, upq, upv,
     tok_all, ten_all, down_all, upq_all, upv_all,
     tok_buf, ten_buf, down_buf, upq_buf, upv_buf,
-    big_s, big_r, small_s, small_r, down_s, down_r, q_s, q_r, v_s, v_r,
+    tok_s, tok_r, down_s, down_r, q_s, q_r, v_s, v_r,
     pq_s, pq_r, pv_s, pv_r, pt_s, pt_r, local_in, local_out,
 ):
     groups, members = sizes
@@ -107,7 +107,7 @@
     gx, gc = grp // nc, grp % nc
     rows = tok.shape[0]
     cols_q = upq.shape[2] // members
-    cut = (rows // (members - 2) // 16 * 16) or 16
+    chunk = rows // tok_s.shape[0]
 
     barrier = pltpu.get_barrier_semaphore()
     for i in range(1, members):
@@ -119,21 +119,22 @@
     def at_tp(first, second):
         return (grp, first * n2 + second)
 
-    def at_tp_swapped(second, first):
-        return (grp, first * n2 + second)
-
     def at_grp(first, second):
         return (first * nc + second, tp)
 
-    big = Chain(
-        n1, n2, a, b, lambda s, t: tok_all.at[s * n2 + t, pl.ds(cut, rows - cut)],
-        tok.at[pl.ds(cut, rows - cut)], big_s, big_r, at_tp,
-    )
-    small = Chain(
-        n2, n1, b, a, lambda t, s: tok_all.at[s * n2 + t, pl.ds(0, cut)],
-        tok.at[pl.ds(0, cut)], small_s, small_r, at_tp_swapped,
-    )
-    downs = Chain(nx, nc, gx, gc, lambda s, t: down_all.at[s * nc + t], down, down_s, down_r, at_grp)
+    def token_chain(c):
+        part = pl.ds(c * chunk, chunk)
+        return Chain(
+            n1, n2, a, b, lambda s, t: tok_all.at[s * n2 + t, part], tok.at[part], tok_s.at[c], tok_r.at[c], at_tp
+        )
+
+    def down_chain(k):
+        return Chain(
+            nx, nc, gx, gc, lambda s, t: down_all.at[s * nc + t, k], down.at[k], down_s.at[k], down_r.at[k], at_grp
+        )
+
+    bigs = [token_chain(c) for c in range(tok_s.shape[0])]
+    downs = [down_chain(k) for k in range(down.shape[0])]
     ups_q = Chain(
         nx, nc, gx, gc, lambda s, t: upq_all.at[s * nc + t], upq_all.at[grp], q_s, q_r, at_grp
     )
@@ -158,12 +159,8 @@
                 send_sem=pt_s.at[j], recv_sem=pt_r.at[src_tp], device_id=dev, device_id_type=MESH),
         )
 
-    small.begin()
-    big.begin()
-    downs.begin()
-    for i in range(1, members):
-        for copy in peers(lax.rem(tp + i, members), tp):
-            copy.start()
+    for chain in bigs + downs:
+        chain.begin()
 
     moves = (
         (columns(upq, cols_q, tp), upq_buf, upq_all.at[grp, tp]),
@@ -180,28 +177,29 @@
     for i, (source, held, target) in enumerate(moves):
         pltpu.make_async_copy(held, target, local_out.at[i]).wait()
 
-    for d in range(1, max(n1, n2) + 1):
-        if d < n1:
-            big.first_step(d)
+    for d in range(1, n1):
+        for chain in bigs:
+            chain.first_step(d)
         if d == 1:
-            for e in range(1, n2):
-                small.first_step(e)
+            for i in range(1, members):
+                for copy in peers(lax.rem(tp + i, members), tp):
+                    copy.start()
+        if d == 2:
+            for chain in downs:
+                for e in range(1, nx):
+                    chain.first_step(e)
             for i in range(1, members):
                 src_tp = lax.rem(tp + i, members)
                 for copy in peers(src_tp, src_tp):
                     copy.wait_recv()
             ups_q.begin()
             ups_v.begin()
-        if 1 < d <= n1:
-            for e in range(n2):
-                small.second_step(e, d - 1)
-    for chain in (downs, ups_q, ups_v):
-        for d in range(1, nx):
-            chain.first_step(d)
-    big.finish_second()
-    for chain in (downs, ups_q, ups_v):
+    for chain in (ups_q, ups_v):
+        for e in range(1, nx):
+            chain.first_step(e)
+    for chain in bigs + downs + [ups_q, ups_v]:
         chain.finish_second()
-    for chain in (big, small, downs, ups_q, ups_v):
+    for chain in bigs + downs + [ups_q, ups_v]:
         chain.drain()
     for i in range(1, members):
         for copy in peers(lax.rem(tp + i, members), tp):
@@ -236,9 +234,9 @@
             pltpu.VMEM(down.shape, BF16),
             pltpu.VMEM((each, rank, cq), BF16),
             pltpu.VMEM((each, rank, cv), BF16),
-            dma((n1, n2, 4)), dma((n1, n2)),
-            dma((n2, n1, 4)), dma((n2, n1)),
-            *grid2, *grid2, *grid2,
+            dma((3, n1, n2, 4)), dma((3, n1, n2)),
+            dma((each, nx, nc, 4)), dma((each, nx, nc)),
+            *grid2, *grid2,
             dma((members,)), dma((members,)), dma((members,)), dma((members,)), dma((members,)), dma((members,)),
             dma((5,)), dma((5,)),
         ],

time: 311 us -> 314 us (level)
    pallas_call x1, Pallas kernels: 176 us -> 193 us  [gather_all(): pl.pallas_call(functools.partial(exchange, (groups, members)), out_shape=...]
    pallas_call x1, Pallas kernels: 79.6 us -> 66.1 us  [finish(): pl.pallas_call(functools.partial(finish_kernel, members, rank), out_shape...]
where the time goes in v4:
time: 314 us; the launch traced here: 313 us
  Pallas kernels  280 us (89%)
  matrix products  24.5 us (8%)
  local copies, waits for them, and re-layouts  7.75 us (2%)
    pallas_call x1, Pallas kernels, gather_all(): pl.pallas_call(functools.partial(exchange, (groups, members)), out_shape=...  193 us
    pallas_call x1, Pallas kernels, finish(): pl.pallas_call(functools.partial(finish_kernel, members, rank), out_shape...  66.1 us
    pallas_call x1, Pallas kernels, down_project(): pl.pallas_call(functools.partial(down_kernel, members), grid=(groups,), o...  20.6 us
    dot_general x1, matrix products, on_device(): base_q = jnp.dot(tok, wq, preferred_element_type=F32)  17.2 us
    dot_general x1, matrix products, on_device(): base_v = jnp.dot(tok, wv, preferred_element_type=F32)  7.28 us

profile of v4, /device:TPU:13, one launch (start us, length us, event | category | flops | bytes accessed | tf_op | source)
XLA Modules:
  0.0 313.3 jit_solution(8258086921475538474)
XLA Ops:
  0.6 0.0 copy-start
  0.6 0.8 add_bitcast_fusion
  1.5 0.7 broadcast_in_dim.9.ten
  2.2 1.7 bitcast_bitcast_fusion.upv
  3.9 192.9 %shard_map.95 = (bf16[8,96,8192]{2,1,0:T(8,128)(2,1)}, s32[8,96,128]{2,1,0:T(8,128)}, bf16[4,2,8192,128]{3,2,1,0:T(8,128)(2,1)}, bf16[4,8,2,64,1024]{4,3,2,1,0:T(8,128)(2,1)}, bf16[4,8,2,64,128]{4,3,2,1,0:T(8,128)(2,1)}) custom-call(bf16[96,8192]{1,0:T(8,128)(2,1)} %tok.1, s32[96,128]{1,0:T(8,128)} %broadcast_in_dim.9.ten, bf16[2,8192,128]{2,1,0:T(8,128)(2,1)} %down.1, ...), custom_call_target="tpu_custom_call" | custom-call | tf_op jit(solution)/shard_map/pallas_call | solution.py:220
  196.8 20.6 %shard_map.96 = bf16[768,128]{1,0:T(8,128)(2,1)} custom-call(bf16[768,8192]{1,0:T(8,128)(2,1)} %bitcast.24, s32[768,128]{1,0:T(8,128)} %bitcast.28, bf16[4,2,8192,128]{3,2,1,0:T(8,128)(2,1)} %get-tuple-element.11.down), custom_call_target="tpu_custom_call" | custom-call | tf_op jit(solution)/shard_map/pallas_call | solution.py:267
  217.4 0.0 copy-start.2
  217.4 0.0 copy-done
  217.4 7.3 %fusion.1.base_v = f32[768,128]{1,0:T(8,128)} fusion(bf16[768,8192]{1,0:T(8,128)(2,1)} %bitcast.25, bf16[8192,128]{1,0:T(8,128)(2,1)S(1)} %copy-done), kind=kOutput, calls=%fused_computation.4 | convolution fusion | flops 1610612736 | bytes 15073280 | tf_op jit(solution)/shard_map/dot_general | solution.py:444
  224.7 1.0 copy-done.2
  225.7 0.0 copy-start.1
  225.7 17.2 %fusion.base_q = f32[768,1024]{1,0:T(8,128)} fusion(bf16[768,8192]{1,0:T(8,128)(2,1)S(1)} %bitcast.26, bf16[8192,1024]{1,0:T(8,128)(2,1)} %param.11), kind=kOutput, calls=%fused_computation.3 | convolution fusion | flops 12884901888 | bytes 32505856 | tf_op jit(solution)/shard_map/dot_general | solution.py:443
  242.9 66.1 %shard_map.97 = (bf16[96,8192]{1,0:T(8,128)(2,1)}, bf16[8,96,128]{2,1,0:T(8,128)(2,1)}) custom-call(bf16[8,96,128]{2,1,0:T(8,128)(2,1)} %bitcast.31, s32[768,128]{1,0:T(8,128)} %bitcast.29, f32[768,1024]{1,0:T(8,128)} %fusion.base_q, f32[768,128]{1,0:T(8,128)} %fusion.1.base_v, bf16[4096,1024]{1,0:T(8,128)(2,1)} %bitcast.27, bf16[4096,128]{1,0:T(8,128)(2,1)} %bitcast.30), custom_call_target="tpu_custom_call" | custom-call | tf_op jit(solution)/shard_map/pallas_call | solution.py:408
  309.1 1.6 copy_bitcast_fusion
  310.7 2.7 copy.17
  313.3 0.0 copy-done.1
Async XLA Ops:
  0.6 216.8 %copy-start = (bf16[8192,128]{1,0:T(8,128)(2,1)S(1)}, bf16[8192,128]{1,0:T(8,128)(2,1)}, u32[]{:S(2)}) copy-start(bf16[8192,128]{1,0:T(8,128)(2,1)} %param.12) | copy-start | bytes 6291460
  217.4 8.3 %copy-start.2 = (bf16[8,96,8192]{2,1,0:T(8,128)(2,1)S(1)}, bf16[8,96,8192]{2,1,0:T(8,128)(2,1)}, u32[]{:S(2)}) copy-start(bf16[8,96,8192]{2,1,0:T(8,128)(2,1)} %get-tuple-element.9) | copy-start | bytes 37748740
  225.7 87.6 %copy-start.1 = (bf16[8192,128]{1,0:T(8,128)(2,1)S(1)}, bf16[8192,128]{1,0:T(8,128)(2,1)}, u32[]{:S(2)}) copy-start(bf16[8192,128]{1,0:T(8,128)(2,1)} %param.12) | copy-start | bytes 6291460
